TPU v7x, 32 devices: a whole 2x2x4 slice. The times are simulated.
32 devices in a mesh: row: 4 (over z), col: 8 (over y, x, core).
Axes of the slice: x: 2, y: 2, z: 4, core: 2. Of those that a mesh axis runs over, the one named last changes fastest.
Arguments:
- trailing: float32 [16384, 16384], P('row', 'col'), may hold values from -51 to 51
- panel_cols: float32 [16384, 128], P(('row', 'col')), as said below
Outputs:
- updated: float32 [16384, 16384], P('row', 'col')
- triangle: float32 [128, 128], replicated
Inputs may be any that keep to these rules, and one draw needn't show every extreme that they name: panel_cols has full column rank.
All inputs are finite; a program needn't handle non-finite values.
Results may differ from a plain program's by a relative error of at most 0.00005.
Values sent between devices are 32-bit elements; how exact they have to be, the bound alone decides.
No kernel may reach another device: no remote copies, remote signals or barrier semaphores. Data moves between devices by JAX's collectives and lax.ppermute only.
A program may use at most 128 MiB of HBM per device.

v0:
```python
import jax
import jax.numpy as jnp
from jax import lax
from jax.sharding import PartitionSpec as P


def spread(array, axis, root):
    mine = lax.axis_index(axis) == root
    return lax.psum(jnp.where(mine, array, jnp.zeros_like(array)), axis)


def matmul(left_side, right_side):
    return jnp.dot(
        left_side, right_side, precision=lax.Precision.HIGHEST, preferred_element_type=jnp.float32
    )


def local(trailing, panel_cols):
    rows_here = trailing.shape[0]
    cols_here = trailing.shape[1]
    blocks_per = rows_here // cols_here
    row_index = lax.axis_index("row")
    col_index = lax.axis_index("col")
    gram_sum = lax.psum(matmul(panel_cols.T, panel_cols), ("row", "col"))
    factor = jnp.linalg.cholesky(gram_sum)
    basis_own = lax.linalg.triangular_solve(factor, panel_cols.T, left_side=True, lower=True).T
    basis_all = lax.all_gather(basis_own, ("row", "col"), axis=0, tiled=True)
    basis_rows = lax.dynamic_slice_in_dim(basis_all, row_index * rows_here, rows_here, 0)
    basis_cols = lax.dynamic_slice_in_dim(basis_all, col_index * cols_here, cols_here, 0)
    partial_value = matmul(trailing, basis_cols)
    image_rows = lax.psum(partial_value, "col")
    coupling = lax.psum(matmul(basis_rows.T, image_rows), "row")
    shift_rows = 2.0 * image_rows - 2.0 * matmul(basis_rows, coupling)
    shift_part = lax.dynamic_slice_in_dim(
        shift_rows, col_index % blocks_per * cols_here, cols_here, 0
    )
    shift_cols = spread(shift_part, "row", col_index // blocks_per)
    left_side = jnp.concatenate([basis_rows, shift_rows], axis=1)
    right_side = jnp.concatenate([shift_cols, basis_cols], axis=1)
    updated = trailing - matmul(left_side, right_side.T)
    return (updated, factor.T)


def solution(mesh):
    in_specs = (P("row", "col"), P(("row", "col"), None))
    out_specs = (P("row", "col"), P())
    return jax.shard_map(local, mesh=mesh, in_specs=in_specs, out_specs=out_specs, check_vma=False)
```

profile of v0, /device:TPU:0, one launch (start us, length us, event | category | flops | bytes accessed | tf_op | source)
XLA Modules:
  0.0 478.7 jit_solution(13148637477328393549)
XLA Ops:
  7.2 0.9 copy-done
  8.1 1.2 fusion.11
  9.4 126.9 %all-reduce.5.cloned.1.call-done = f32[128,128]{0,1:T(8,128)} async-done(((f32[128,128]{0,1:T(8,128)}), f32[128,128]{0,1:T(8,128)}) %all-reduce.5.cloned.1.call-update) | async-done | bytes 65552 | tf_op jit(solution)/shard_map/psum | solution.py:24
  136.3 0.9 copy.5
  137.2 0.9 fusion.8
  138.1 11.7 %cholesky.16 = f32[128,128]{1,0:T(8,128)S(1)} custom-call(f32[128,128]{1,0:T(8,128)S(1)} %fusion.8), custom_call_target="Cholesky" | custom-call | tf_op jit(solution)/shard_map/jit(cholesky)/cholesky | solution.py:25
  149.8 0.6 compare_reduce_fusion
  150.5 0.7 fusion.9
  151.1 9.8 %custom-call.6 = f32[1,128,128]{1,2,0:T(8,128)S(1)} custom-call(f32[1,128,128]{2,1,0:T(8,128)S(1)} %get-tuple-element.5), custom_call_target="InvertDiagBlocksLowerTriangular" | custom-call | tf_op jit(solution)/shard_map/triangular_solve | solution.py:26
  160.9 1.1 convolution_bitcast_fusion.1
  162.3 78.6 %all-gather.2.cloned.1.call-done = f32[16384,128]{0,1:T(8,128)} async-done(((f32[512,128]{0,1:T(8,128)}), f32[16384,128]{0,1:T(8,128)}) %all-gather.2.cloned.1.call-update) | async-done | bytes 8388624 | tf_op jit(solution)/shard_map/all_gather | solution.py:27
  240.9 1.3 constant_dynamic-slice_fusion
  242.2 38.6 %convolution_bitcast_fusion = f32[4096,128]{0,1:T(8,128)} fusion(f32[2048,128]{0,1:T(8,128)S(1)} %constant_dynamic-slice_fusion, f32[4096,2048]{1,0:T(8,128)} %param.2), kind=kOutput, calls=%fused_computation.3 | convolution fusion | flops 12884901888 | bytes 36700160 | tf_op jit(solution)/shard_map/dot_general | solution.py:13
  280.9 1.7 constant_dynamic-slice_fusion.1
  282.7 59.4 %all-reduce.7.cloned.1.call-done = f32[4096,128]{0,1:T(8,128)} async-done(((f32[4096,128]{0,1:T(8,128)}), f32[4096,128]{0,1:T(8,128)}) %all-reduce.7.cloned.1.call-update) | async-done | bytes 2097168 | tf_op jit(solution)/shard_map/psum | solution.py:31
  342.0 4.1 fusion.12
  346.1 0.3 all-reduce.11.cloned.1.call-start
  346.4 33.2 %all-reduce.9.cloned.1.call-done = f32[128,128]{1,0:T(8,128)} async-done(((f32[128,128]{1,0:T(8,128)}), f32[128,128]{1,0:T(8,128)}) %all-reduce.9.cloned.1.call-update) | async-done | bytes 65552 | tf_op jit(solution)/shard_map/psum | solution.py:32
  379.6 3.8 fusion
  383.4 1.3 copy-done.2
  384.8 1.0 dynamic-slice_select_fusion
  385.8 0.7 copy.6
  386.6 51.0 %all-reduce.11.cloned.1.call-done = f32[2048,128]{0,1:T(8,128)} async-done(((f32[2048,128]{0,1:T(8,128)}), f32[2048,128]{0,1:T(8,128)}) %all-reduce.11.cloned.1.call-update) | async-done | bytes 1048592 | tf_op jit(solution)/shard_map/psum | solution.py:9
  437.6 34.6 %convolution_subtract_fusion = f32[4096,2048]{1,0:T(8,128)} fusion(f32[4096,2048]{1,0:T(8,128)} %param.2, f32[4096,128]{0,1:T(8,128)} %copy-done.2, f32[4096,128]{0,1:T(8,128)S(1)} %constant_dynamic-slice_fusion.1, f32[2048,128]{0,1:T(8,128)S(1)} %constant_dynamic-slice_fusion, f32[2048,128]{0,1:T(8,128)} %all-reduce.11.cloned.1.call-done), kind=kOutput, calls=%fused_computation | convolution fusion | flops 25779765248 | bytes 73400320 | tf_op jit(solution)/shard_map/dot_general | solution.py:13
  (14 shorter events, 0.5 us)
Async XLA Ops:
  7.2 1.0 copy-start
  7.2 129.1 %all-reduce.5.cloned.1.call-start = ((), (), s32[]{:S(2)}) async-start(), calls=%async_computation | async-start | bytes 131072 | tf_op jit(solution)/shard_map/psum | solution.py:24
  9.4 231.6 %all-gather.2.cloned.1.call-start = ((), (), s32[]{:S(2)}) async-start(), calls=%async_computation.1 | async-start | bytes 8650752 | tf_op jit(solution)/shard_map/all_gather | solution.py:27
  162.1 179.9 %all-reduce.7.cloned.1.call-start = ((), (), s32[]{:S(2)}) async-start(), calls=%async_computation.2 | async-start | bytes 4194304 | tf_op jit(solution)/shard_map/psum | solution.py:31
  280.8 98.8 %all-reduce.9.cloned.1.call-start = ((), (), s32[]{:S(2)}) async-start(), calls=%async_computation.3 | async-start | bytes 131072 | tf_op jit(solution)/shard_map/psum | solution.py:32
  346.1 91.5 %all-reduce.11.cloned.1.call-start = ((), (), s32[]{:S(2)}) async-start(), calls=%async_computation.4 | async-start | bytes 2097152 | tf_op jit(solution)/shard_map/psum | solution.py:9
  383.4 1.3 copy-start.2
  437.6 34.6 %copy-start.1 = (f32[512,128]{1,0:T(8,128)S(1)}, f32[512,128]{1,0:T(8,128)}, u32[]{:S(2)}) copy-start(f32[512,128]{1,0:T(8,128)} %param.3) | copy-start | bytes 786436
Sparse Core Ops, SparseCore 0:
  14.1 122.0 all-reduce.4
  162.2 78.6 all-gather.1
  281.0 60.9 all-reduce.6
  346.2 33.3 all-reduce.8
  386.0 51.5 all-reduce.10
where the time goes:
time: 479 us
  waiting for transfers between devices  349 us (73%)
  matrix products  83.4 us (17%)
  other arithmetic  24.8 us (5%)
  between operations  13.9 us (3%)
  local copies, waits for them, and re-layouts  6.96 us (1%)
    psum x1, waiting for transfers between devices, local(): gram_sum = lax.psum(matmul(panel_cols.T, panel_cols), ('row', 'col'))  127 us
    dot_general x5, matrix products, matmul(): jnp.dot(left_side, right_side, precision=lax.Precision.HIGHEST, preferred...  82.2 us
    all_gather x1, waiting for transfers between devices, local(): basis_all = lax.all_gather(basis_own, ('row', 'col'), axis=0, tiled=True)  78.6 us
    psum x1, waiting for transfers between devices, local(): image_rows = lax.psum(partial_value, 'col')  59.4 us
    psum x1, waiting for transfers between devices, spread(): return lax.psum(jnp.where(mine, array, jnp.zeros_like(array)), axis)  51 us
    psum x1, waiting for transfers between devices, local(): coupling = lax.psum(matmul(basis_rows.T, image_rows), 'row')  33.2 us
    another operation x3, other arithmetic, local(): factor = jnp.linalg.cholesky(gram_sum)  12.4 us
    another operation x1, other arithmetic, local(): lax.linalg.triangular_solve(factor, panel_cols.T, left_side=True, lower=T...  9.81 us
  transfers between devices with their start and end apart: 5, of which 5 were waited for; matrix products, arithmetic and copies ran while one was open for 1% of the time, Pallas kernels for 0%

commit v1 on v0

--- a/solution.py
+++ b/solution.py
@@ -29,7 +29,9 @@
     basis_cols = lax.dynamic_slice_in_dim(basis_all, col_index * cols_here, cols_here, 0)
     partial_value = matmul(trailing, basis_cols)
     image_rows = lax.psum(partial_value, "col")
-    coupling = lax.psum(matmul(basis_rows.T, image_rows), "row")
+    content = matmul(basis_rows.T, image_rows)
+    after = lax.all_gather(content, axis_name="row")
+    coupling = jnp.sum(after, axis=0)
     shift_rows = 2.0 * image_rows - 2.0 * matmul(basis_rows, coupling)
     shift_part = lax.dynamic_slice_in_dim(
         shift_rows, col_index % blocks_per * cols_here, cols_here, 0

time: 479 us -> 459 us (0.958)
  waiting for transfers between devices: 349 us -> 316 us
  blocking collectives: 0 us -> 14.2 us
    psum x1 -> x0, waiting for transfers between devices: 33.2 us -> none  [local(): coupling = lax.psum(matmul(basis_rows.T, image_rows), 'row')]
    all_gather x0 -> x1, blocking collectives: none -> 14.2 us  [local(): after = lax.all_gather(content, axis_name='row')]
  transfers between devices with their start and end apart: 5 -> 4, of which waited for: 5 -> 4; matrix products, arithmetic and copies ran while one was open for 1% -> 1% of each run, Pallas kernels for 0% -> 0%
where the time goes in v1:
time: 459 us
  waiting for transfers between devices  316 us (69%)
  matrix products  82.7 us (18%)
  other arithmetic  24.8 us (5%)
  blocking collectives  14.2 us (3%)
  between operations  13.9 us (3%)
  local copies, waits for them, and re-layouts  6.97 us (2%)
    psum x1, waiting for transfers between devices, local(): gram_sum = lax.psum(matmul(panel_cols.T, panel_cols), ('row', 'col'))  127 us
    dot_general x5, matrix products, matmul(): jnp.dot(left_side, right_side, precision=lax.Precision.HIGHEST, preferred...  81.5 us
    all_gather x1, waiting for transfers between devices, local(): basis_all = lax.all_gather(basis_own, ('row', 'col'), axis=0, tiled=True)  78.6 us
    psum x1, waiting for transfers between devices, local(): image_rows = lax.psum(partial_value, 'col')  59.4 us
    psum x1, waiting for transfers between devices, spread(): return lax.psum(jnp.where(mine, array, jnp.zeros_like(array)), axis)  51 us
    all_gather x1, blocking collectives, local(): after = lax.all_gather(content, axis_name='row')  14.2 us
    another operation x3, other arithmetic, local(): factor = jnp.linalg.cholesky(gram_sum)  12.4 us
    another operation x1, other arithmetic, local(): lax.linalg.triangular_solve(factor, panel_cols.T, left_side=True, lower=T...  9.81 us
  transfers between devices with their start and end apart: 4, of which 4 were waited for; matrix products, arithmetic and copies ran while one was open for 1% of the time, Pallas kernels for 0%

profile of v1, /device:TPU:0, one launch (start us, length us, event | category | flops | bytes accessed | tf_op | source)
XLA Modules:
  0.0 458.7 jit_solution(82577340016183719)
XLA Ops:
  7.2 0.9 copy-done
  8.1 1.2 fusion.11
  9.4 126.9 %all-reduce.4.cloned.1.call-done = f32[128,128]{0,1:T(8,128)} async-done(((f32[128,128]{0,1:T(8,128)}), f32[128,128]{0,1:T(8,128)}) %all-reduce.4.cloned.1.call-update) | async-done | bytes 65552 | tf_op jit(solution)/shard_map/psum | solution.py:24
  136.3 0.9 copy.5
  137.2 0.9 fusion.8
  138.1 11.7 %cholesky.16 = f32[128,128]{1,0:T(8,128)S(1)} custom-call(f32[128,128]{1,0:T(8,128)S(1)} %fusion.8), custom_call_target="Cholesky" | custom-call | tf_op jit(solution)/shard_map/jit(cholesky)/cholesky | solution.py:25
  149.8 0.6 compare_reduce_fusion
  150.5 0.7 fusion.9
  151.1 9.8 %custom-call.6 = f32[1,128,128]{1,2,0:T(8,128)S(1)} custom-call(f32[1,128,128]{2,1,0:T(8,128)S(1)} %get-tuple-element.5), custom_call_target="InvertDiagBlocksLowerTriangular" | custom-call | tf_op jit(solution)/shard_map/triangular_solve | solution.py:26
  160.9 1.1 convolution_bitcast_fusion.1
  162.1 0.2 all-reduce.6.cloned.1.call-start
  162.3 78.6 %all-gather.3.cloned.1.call-done = f32[16384,128]{0,1:T(8,128)} async-done(((f32[512,128]{0,1:T(8,128)}), f32[16384,128]{0,1:T(8,128)}) %all-gather.3.cloned.1.call-update) | async-done | bytes 8388624 | tf_op jit(solution)/shard_map/all_gather | solution.py:27
  240.9 1.3 constant_dynamic-slice_fusion
  242.3 38.6 %convolution_bitcast_fusion = f32[4096,128]{0,1:T(8,128)} fusion(f32[2048,128]{0,1:T(8,128)S(1)} %constant_dynamic-slice_fusion, f32[4096,2048]{1,0:T(8,128)} %param.2), kind=kOutput, calls=%fused_computation.3 | convolution fusion | flops 12884901888 | bytes 36700160 | tf_op jit(solution)/shard_map/dot_general | solution.py:13
  280.9 1.7 constant_dynamic-slice_fusion.1
  282.7 59.4 %all-reduce.6.cloned.1.call-done = f32[4096,128]{0,1:T(8,128)} async-done(((f32[4096,128]{0,1:T(8,128)}), f32[4096,128]{0,1:T(8,128)}) %all-reduce.6.cloned.1.call-update) | async-done | bytes 2097168 | tf_op jit(solution)/shard_map/psum | solution.py:31
  342.0 3.4 fusion.12
  345.5 14.2 %all-gather = f32[512,128]{1,0:T(8,128)S(1)} all-gather(f32[128,128]{1,0:T(8,128)S(1)} %fusion.12), channel_id=2, replica_groups=mesh['row'=4,'col'=8] {'row'}, dimensions={0}, use_global_device_ids=true | all-gather | bytes 327680 | tf_op jit(solution)/shard_map/all_gather | solution.py:33
  359.6 3.8 fusion
  363.4 1.3 copy-done.2
  364.8 1.0 dynamic-slice_select_fusion
  365.8 0.7 copy.6
  366.6 51.0 %all-reduce.8.cloned.1.call-done = f32[2048,128]{0,1:T(8,128)} async-done(((f32[2048,128]{0,1:T(8,128)}), f32[2048,128]{0,1:T(8,128)}) %all-reduce.8.cloned.1.call-update) | async-done | bytes 1048592 | tf_op jit(solution)/shard_map/psum | solution.py:9
  417.6 34.6 %convolution_subtract_fusion = f32[4096,2048]{1,0:T(8,128)} fusion(f32[4096,2048]{1,0:T(8,128)} %param.2, f32[4096,128]{0,1:T(8,128)} %copy-done.2, f32[4096,128]{0,1:T(8,128)S(1)} %constant_dynamic-slice_fusion.1, f32[2048,128]{0,1:T(8,128)S(1)} %constant_dynamic-slice_fusion, f32[2048,128]{0,1:T(8,128)} %all-reduce.8.cloned.1.call-done), kind=kOutput, calls=%fused_computation | convolution fusion | flops 25779765248 | bytes 73400320 | tf_op jit(solution)/shard_map/dot_general | solution.py:13
  (13 shorter events, 0.3 us)
Async XLA Ops:
  7.2 1.0 copy-start
  7.2 129.1 %all-reduce.4.cloned.1.call-start = ((), (), s32[]{:S(2)}) async-start(), calls=%async_computation | async-start | bytes 131072 | tf_op jit(solution)/shard_map/psum | solution.py:24
  9.4 231.6 %all-gather.3.cloned.1.call-start = ((), (), s32[]{:S(2)}) async-start(), calls=%async_computation.1 | async-start | bytes 8650752 | tf_op jit(solution)/shard_map/all_gather | solution.py:27
  162.1 179.9 %all-reduce.6.cloned.1.call-start = ((), (), s32[]{:S(2)}) async-start(), calls=%async_computation.2 | async-start | bytes 4194304 | tf_op jit(solution)/shard_map/psum | solution.py:31
  280.9 136.7 %all-reduce.8.cloned.1.call-start = ((), (), s32[]{:S(2)}) async-start(), calls=%async_computation.3 | async-start | bytes 2097152 | tf_op jit(solution)/shard_map/psum | solution.py:9
  363.4 1.4 copy-start.2
  417.6 34.6 %copy-start.1 = (f32[512,128]{1,0:T(8,128)S(1)}, f32[512,128]{1,0:T(8,128)}, u32[]{:S(2)}) copy-start(f32[512,128]{1,0:T(8,128)} %param.3) | copy-start | bytes 786436
Sparse Core Ops, SparseCore 0:
  14.1 122.0 all-reduce.3
  162.2 78.6 all-gather.2
  281.0 61.0 all-reduce.5
  366.0 51.5 all-reduce.7
